TPU v7x, 256 devices: a whole 4x4x8 slice. The times are simulated.
256 devices in a mesh: wide: 64 (over y, z, core), narrow: 4 (over x).
Axes of the slice: x: 4, y: 4, z: 8, core: 2. Of those that a mesh axis runs over, the one named last changes fastest.
Arguments:
- features: bfloat16 [768, 524288], P('narrow', 'wide'), may hold values from -6 to 6
- owner_of: int32 [32768, 16, 1], P('wide'), may hold values from 0 to 63; in each aligned block of 8192 rows (0 to 8191, 8192 to 16383, ..., all dimensions but the last counted through in order) at most 192 rows name the same one
- row_of: int32 [32768, 16], P('wide'), may hold values from 0 to 8191
- w_self: bfloat16 [768, 256], P('narrow'), may hold values from -0.15625 to 0.15625
- w_neighbor: bfloat16 [768, 256], P('narrow'), may hold values from -0.15625 to 0.15625
- cotangent: bfloat16 [32768, 256], P(('wide', 'narrow')), may hold values from -0.032958984 to 0.032958984
Outputs:
- hidden: bfloat16 [32768, 256], P(('wide', 'narrow'))
- grad_self: float32 [768, 256], P('narrow')
- grad_neighbor: float32 [768, 256], P('narrow')
Inputs may be any that keep to these rules, and one draw needn't show every extreme that they name: `owner_of`: among the 8192 rows read by the targets of one index of wide, no owner is named more than 192 times, and in every draw some owner is named exactly 192 times by some index.
All inputs are finite; a program needn't handle non-finite values.
Results may differ from a plain program's by a relative error of at most 0.0054.
Values may be sent and summed in bfloat16 or wider, within the bound.
A program may use at most 64 MiB of HBM per device.

v0:
```python
import jax
import jax.numpy as jnp
from jax import lax
from jax.sharding import PartitionSpec as P

FANOUT = 15


def activation(value):
    return jax.nn.gelu(value, approximate=True)


def contract_rows(left, right):
    return lax.dot_general(
        left, right, (((0,), (0,)), ((), ())), preferred_element_type=jnp.float32
    )


def slot_numbers(owners, wide_count, total):
    block_rows = 128
    block_count = total // block_rows
    onehot = (owners[:, None] == jnp.arange(wide_count, dtype=jnp.int32)[None, :]).astype(
        jnp.float32
    )
    blocked = onehot.reshape(block_count, block_rows, wide_count)
    lower = (jnp.arange(block_rows)[:, None] > jnp.arange(block_rows)[None, :]).astype(jnp.float32)
    within = jnp.einsum("ij,bjw->biw", lower, blocked, precision=lax.Precision.HIGHEST)
    block_sums = jnp.sum(blocked, axis=1)
    offsets = jnp.cumsum(block_sums, axis=0) - block_sums
    prefix = within + offsets[:, None, :]
    return jnp.sum(prefix * blocked, axis=2).reshape(total).astype(jnp.int32)


def on_device(features, owner_of, row_of, w_self, w_neighbor, cotangent):
    wide_count = lax.axis_size("wide")
    narrow_count = lax.axis_size("narrow")
    tgt_rows, request_count = row_of.shape
    feat_cols = features.shape[0]
    total = tgt_rows * request_count
    capacity = max(2, 3 * total // (2 * wide_count))
    owners = owner_of.reshape(total)
    wanted = row_of.reshape(total)
    slot_of = slot_numbers(owners, wide_count, total)
    flat_slot = owners * capacity + slot_of
    buffer = (
        jnp.zeros((wide_count * capacity,), jnp.int32)
        .at[flat_slot]
        .set(wanted)
        .reshape(wide_count, capacity)
    )
    table = jnp.transpose(features)
    found = jnp.take(
        table, lax.all_to_all(buffer, "wide", split_axis=0, concat_axis=0, tiled=True), axis=0
    )
    fetched = lax.all_to_all(found, "wide", split_axis=0, concat_axis=0, tiled=True)
    flat_fetched = fetched.reshape(wide_count * capacity, feat_cols)
    gathered = jnp.take(flat_fetched, flat_slot, axis=0).reshape(tgt_rows, request_count, feat_cols)
    self_rows = gathered[:, 0]
    pooled = (jnp.sum(gathered[:, 1:], axis=1, dtype=jnp.float32) / FANOUT).astype(jnp.bfloat16)
    share = tgt_rows // narrow_count
    preact = lax.psum(
        jnp.dot(self_rows, w_self, preferred_element_type=jnp.float32)
        + jnp.dot(pooled, w_neighbor, preferred_element_type=jnp.float32),
        "narrow",
    )
    value, pullback = jax.vjp(activation, preact)
    full_cot = lax.all_gather(cotangent, "narrow", axis=0, tiled=True)
    slope = pullback(full_cot.astype(jnp.float32))[0].astype(jnp.bfloat16)
    mine = lax.axis_index("narrow") * share
    hidden = lax.dynamic_slice_in_dim(value, mine, share, 0).astype(jnp.bfloat16)
    grad_self, grad_neighbor = lax.psum(
        (contract_rows(self_rows, slope), contract_rows(pooled, slope)), "wide"
    )
    return (hidden, grad_self, grad_neighbor)


def solution(mesh):
    return jax.shard_map(
        on_device,
        mesh=mesh,
        in_specs=(
            P("narrow", "wide"),
            P("wide", None, None),
            P("wide", None),
            P("narrow", None),
            P("narrow", None),
            P(("wide", "narrow"), None),
        ),
        out_specs=(P(("wide", "narrow"), None), P("narrow", None), P("narrow", None)),
        check_vma=False,
    )
```

profile of v0, /device:TPU:2, one launch (start us, length us, event | category | flops | bytes accessed | tf_op | source)
XLA Modules:
  0.0 561.9 jit_solution(12965184154446572540)
XLA Ops:
  7.2 1.0 copy.24
  8.2 1.4 copy_multiply_fusion
  9.7 0.6 convert_reduce_fusion.1
  10.5 0.8 fusion
  11.3 0.9 copy.26
  12.2 0.8 mul.76
  13.0 0.9 copy.27
  13.9 0.7 reshape.155
  14.6 0.8 compare_select_fusion.1
  15.4 30.7 %scatter_custom_fusion = s32[12288]{0:T(1024)S(1)} fusion(s32[8192]{0:T(1024)S(1)} %bitcast.41, s32[8192]{0:T(1024)} %reshape.155, s32[]{:T(128)} %constant.21.clone.1), kind=kCustom, calls=%fused_computation.47 | custom fusion | bytes 49664 | tf_op jit(solution)/shard_map/scatter | solution.py:48
  46.1 0.8 all_to_all.13
  46.9 12.1 %all-to-all-start = ((s32[64,1,192]{2,1,0:T(1,128)}), s32[64,1,192]{2,1,0:T(1,128)S(1)}, u32[]{:S(2)}, u32[]{:S(2)}) async-start(s32[64,1,192]{2,1,0:T(1,128)} %all_to_all.13), calls=%async_computation | async-start | bytes 131072 | tf_op jit(solution)/shard_map/all_to_all | solution.py:53
  59.0 4.0 copy.28
  63.0 5.7 %all-to-all-done = s32[64,1,192]{2,1,0:T(1,128)S(1)} async-done(((s32[64,1,192]{2,1,0:T(1,128)}), s32[64,1,192]{2,1,0:T(1,128)S(1)}, u32[]{:S(2)}, u32[]{:S(2)}) %all-to-all-start) | async-done | bytes 49184 | tf_op jit(solution)/shard_map/all_to_all | solution.py:53
  69.0 48.5 %gather_fusion = bf16[12288,192]{1,0:T(8,128)(2,1)} fusion(bf16[8192,192]{1,0:T(8,128)(2,1)} %bitcast.37, s32[12288]{0:T(1024)S(1)} %broadcast_clamp_fusion), kind=kCustom, calls=%fused_computation | custom fusion | bytes 9486336 | tf_op jit(solution)/shard_map/jit(_take)/gather | solution.py:52
  117.6 7.6 %broadcast_select_fusion = bf16[64,192,192]{2,1,0:T(8,128)(2,1)} fusion(bf16[64,192,192]{2,1,0:T(8,128)(2,1)} %bitcast.38, pred[64,192]{1,0:T(8,128)(4,1)S(1)} %compare_and_fusion), kind=kLoop, calls=%fused_computation.3 | loop fusion | flops 2359296 | bytes 9449472 | tf_op jit(solution)/shard_map/jit(_take)/select_n | solution.py:52
  125.2 5.8 %all-to-all-start.1 = ((bf16[64,192,192]{2,1,0:T(8,128)(2,1)}), bf16[64,192,192]{2,1,0:T(8,128)(2,1)}, u32[]{:S(2)}, u32[]{:S(2)}) async-start(bf16[64,192,192]{2,1,0:T(8,128)(2,1)} %broadcast_select_fusion), calls=%async_computation.1 | async-start | bytes 12582912 | tf_op jit(solution)/shard_map/all_to_all | solution.py:55
  131.4 139.8 %all-to-all-done.1 = bf16[64,192,192]{2,1,0:T(8,128)(2,1)} async-done(((bf16[64,192,192]{2,1,0:T(8,128)(2,1)}), bf16[64,192,192]{2,1,0:T(8,128)(2,1)}, u32[]{:S(2)}, u32[]{:S(2)}) %all-to-all-start.1) | async-done | bytes 4718624 | tf_op jit(solution)/shard_map/all_to_all | solution.py:55
  271.2 34.5 %gather_fusion.1 = bf16[8192,192]{1,0:T(8,128)(2,1)} fusion(bf16[12288,192]{1,0:T(8,128)(2,1)} %bitcast.8, s32[8192]{0:T(1024)S(1)} %broadcast_clamp_fusion.1), kind=kCustom, calls=%fused_computation.1 | custom fusion | bytes 6324224 | tf_op jit(solution)/shard_map/jit(_take)/gather | solution.py:57
  305.7 7.7 %copy.29 = bf16[512,16,192]{0,2,1:T(8,128)(2,1)} copy(bf16[512,16,192]{2,1,0:T(8,128)(2,1)} %bitcast.39) | data formatting | bytes 6291456 | tf_op jit(solution)/shard_map/jit(_take)/gather | solution.py:57
  313.4 2.2 broadcast_select_fusion.1
  316.3 0.5 copy-done.1
  316.8 1.1 convolution_add_fusion
  317.9 12.5 %all_gather.3 = bf16[512,256]{1,0:T(8,128)(2,1)S(1)} all-gather(bf16[128,256]{1,0:T(8,128)(2,1)} %param.11), channel_id=1, replica_groups=mesh['wide'=64,'narrow'=4] {'narrow'}, dimensions={0}, use_global_device_ids=true | all-gather | bytes 327680 | tf_op jit(solution)/shard_map/all_gather | solution.py:67
  330.5 32.0 %all-reduce.4.cloned.1.call-done = f32[512,256]{1,0:T(8,128)} async-done(((f32[512,256]{1,0:T(8,128)}), f32[512,256]{1,0:T(8,128)}) %all-reduce.4.cloned.1.call-update) | async-done | bytes 524304 | tf_op jit(solution)/shard_map/psum | solution.py:61
  362.5 2.2 fusion.5
  364.7 1.9 fusion.16
  366.6 0.9 fusion.13
  367.5 1.6 fusion.15
  369.1 182.7 %all-reduce.6.cloned.1.call-done = (f32[192,256]{1,0:T(8,128)}, f32[192,256]{1,0:T(8,128)}) async-done(((f32[192,256]{1,0:T(8,128)}, f32[192,256]{1,0:T(8,128)}), (f32[192,256]{1,0:T(8,128)}, f32[192,256]{1,0:T(8,128)})) %all-reduce.6.cloned.1.call-update) | async-done | bytes 393232 | tf_op jit(solution)/shard_map/psum | solution.py:71
  551.9 1.6 copy.40
  553.5 1.6 copy.41
  (27 shorter events, 1.6 us)
Async XLA Ops:
  7.2 308.9 %copy-start = (bf16[192,256]{1,0:T(8,128)(2,1)S(1)}, bf16[192,256]{1,0:T(8,128)(2,1)}, u32[]{:S(2)}) copy-start(bf16[192,256]{1,0:T(8,128)(2,1)} %param.9) | copy-start | bytes 294916
  7.2 51.8 %copy-start.2 = (bf16[192,8192]{1,0:T(8,128)(2,1)S(1)}, bf16[192,8192]{1,0:T(8,128)(2,1)}, u32[]{:S(2)}) copy-start(bf16[192,8192]{1,0:T(8,128)(2,1)} %param.6) | copy-start | bytes 9437188
  46.9 21.8 %all-to-all-start = ((s32[64,1,192]{2,1,0:T(1,128)}), s32[64,1,192]{2,1,0:T(1,128)S(1)}, u32[]{:S(2)}, u32[]{:S(2)}) async-start(s32[64,1,192]{2,1,0:T(1,128)} %all_to_all.13), calls=%async_computation | async-start | bytes 131072 | tf_op jit(solution)/shard_map/all_to_all | solution.py:53
  125.2 6.1 %copy-start.3 = (s32[512,16,1]{0,2,1:T(1,128)S(1)}, s32[512,16,1]{0,2,1:T(1,128)}, u32[]{:S(2)}) copy-start(s32[512,16,1]{0,2,1:T(1,128)} %param.7) | copy-start | bytes 98308
  125.2 146.0 %all-to-all-start.1 = ((bf16[64,192,192]{2,1,0:T(8,128)(2,1)}), bf16[64,192,192]{2,1,0:T(8,128)(2,1)}, u32[]{:S(2)}, u32[]{:S(2)}) async-start(bf16[64,192,192]{2,1,0:T(8,128)(2,1)} %broadcast_select_fusion), calls=%async_computation.1 | async-start | bytes 12582912 | tf_op jit(solution)/shard_map/all_to_all | solution.py:55
  131.0 231.5 %all-reduce.4.cloned.1.call-start = ((), (), s32[]{:S(2)}) async-start(), calls=%async_computation.2 | async-start | bytes 1048576 | tf_op jit(solution)/shard_map/psum | solution.py:61
  315.6 1.2 copy-start.4
  316.0 0.7 copy-start.1
  317.9 234.0 %all-reduce.6.cloned.1.call-start = ((), (), s32[]{:S(2)}) async-start(), calls=%async_computation.3 | async-start | bytes 786432 | tf_op jit(solution)/shard_map/psum | solution.py:71
Sparse Core Ops, SparseCore 0:
  318.0 44.4 all-reduce.3
  367.6 184.1 all-reduce.5
where the time goes:
time: 563 us; the launch traced here: 562 us
  waiting for transfers between devices  360 us (64%)
  local copies, waits for them, and re-layouts  135 us (24%)
  starting transfers between devices  18 us (3%)
  other arithmetic  17.3 us (3%)
  between operations  14.2 us (3%)
  blocking collectives  12.5 us (2%)
    psum x1, waiting for transfers between devices, on_device(): lax.psum((contract_rows(self_rows, slope), contract_rows(pooled, slope)),...  183 us
    all_to_all x1, waiting for transfers between devices, on_device(): lax.all_to_all(found, 'wide', split_axis=0, concat_axis=0, tiled=True)  140 us
    gather x1, local copies, waits for them, and re-layouts, on_device(): jnp.take(table, lax.all_to_all(buffer, 'wide', split_axis=0, concat_axis=...  48.5 us
    gather x2, local copies, waits for them, and re-layouts, on_device(): jnp.take(flat_fetched, flat_slot, axis=0)  42.2 us
    psum x1, waiting for transfers between devices, on_device(): lax.psum(jnp.dot(self_rows, w_self, preferred_element_type=jnp.float32) +...  32 us
    scatter x1, local copies, waits for them, and re-layouts, on_device(): buffer = jnp.zeros((wide_count * capacity,), jnp.int32).at[flat_slot].set...  30.7 us
    all_gather x1, blocking collectives, on_device(): full_cot = lax.all_gather(cotangent, 'narrow', axis=0, tiled=True)  12.5 us
    all_to_all x1, starting transfers between devices, on_device(): lax.all_to_all(buffer, 'wide', split_axis=0, concat_axis=0, tiled=True)  12.1 us
  transfers between devices with their start and end apart: 4, of which 4 were waited for; matrix products, arithmetic and copies ran while one was open for 1% of the time, Pallas kernels for 0%

commit v1 on v0

--- a/solution.py
+++ b/solution.py
@@ -58,10 +58,13 @@
     self_rows = gathered[:, 0]
     pooled = (jnp.sum(gathered[:, 1:], axis=1, dtype=jnp.float32) / FANOUT).astype(jnp.bfloat16)
     share = tgt_rows // narrow_count
-    preact = lax.psum(
-        jnp.dot(self_rows, w_self, preferred_element_type=jnp.float32)
-        + jnp.dot(pooled, w_neighbor, preferred_element_type=jnp.float32),
-        "narrow",
+    preact = jnp.sum(
+        lax.all_gather(
+            jnp.dot(self_rows, w_self, preferred_element_type=jnp.float32)
+            + jnp.dot(pooled, w_neighbor, preferred_element_type=jnp.float32),
+            "narrow",
+        ),
+        axis=0,
     )
     value, pullback = jax.vjp(activation, preact)
     full_cot = lax.all_gather(cotangent, "narrow", axis=0, tiled=True)

time: 563 us -> 550 us (0.977)
  waiting for transfers between devices: 360 us -> 344 us
    psum x1 -> x0, waiting for transfers between devices: 32 us -> none  [on_device(): lax.psum(jnp.dot(self_rows, w_self, preferred_element_type=jnp.float32) +...]
    all_gather x0 -> x1, waiting for transfers between devices: none -> 16.7 us  [on_device(): lax.all_gather(jnp.dot(self_rows, w_self, preferred_element_type=jnp.floa...]
where the time goes in v1:
time: 550 us; the launch traced here: 549 us
  waiting for transfers between devices  344 us (63%)
  local copies, waits for them, and re-layouts  135 us (25%)
  other arithmetic  19.8 us (4%)
  starting transfers between devices  18 us (3%)
  between operations  14.2 us (3%)
  blocking collectives  13 us (2%)
    psum x1, waiting for transfers between devices, on_device(): lax.psum((contract_rows(self_rows, slope), contract_rows(pooled, slope)),...  182 us
    all_to_all x1, waiting for transfers between devices, on_device(): lax.all_to_all(found, 'wide', split_axis=0, concat_axis=0, tiled=True)  140 us
    gather x1, local copies, waits for them, and re-layouts, on_device(): jnp.take(table, lax.all_to_all(buffer, 'wide', split_axis=0, concat_axis=...  48.5 us
    gather x2, local copies, waits for them, and re-layouts, on_device(): jnp.take(flat_fetched, flat_slot, axis=0)  42.2 us
    scatter x1, local copies, waits for them, and re-layouts, on_device(): buffer = jnp.zeros((wide_count * capacity,), jnp.int32).at[flat_slot].set...  30.7 us
    all_gather x1, waiting for transfers between devices, on_device(): lax.all_gather(jnp.dot(self_rows, w_self, preferred_element_type=jnp.floa...  16.7 us
    all_gather x1, blocking collectives, on_device(): full_cot = lax.all_gather(cotangent, 'narrow', axis=0, tiled=True)  13 us
    all_to_all x1, starting transfers between devices, on_device(): lax.all_to_all(buffer, 'wide', split_axis=0, concat_axis=0, tiled=True)  12.1 us
  transfers between devices with their start and end apart: 4, of which 4 were waited for; matrix products, arithmetic and copies ran while one was open for 1% of the time, Pallas kernels for 0%

profile of v1, /device:TPU:2, one launch (start us, length us, event | category | flops | bytes accessed | tf_op | source)
XLA Modules:
  0.0 549.2 jit_solution(1189586559757823041)
XLA Ops:
  7.2 1.0 copy.24
  8.2 1.4 copy_multiply_fusion
  9.7 0.6 convert_reduce_fusion.1
  10.5 0.8 fusion
  11.3 0.9 copy.26
  12.2 0.8 mul.76
  13.0 0.9 copy.27
  13.9 0.7 reshape.155
  14.6 0.8 compare_select_fusion.1
  15.4 30.7 %scatter_custom_fusion = s32[12288]{0:T(1024)S(1)} fusion(s32[8192]{0:T(1024)S(1)} %bitcast.43, s32[8192]{0:T(1024)} %reshape.155, s32[]{:T(128)} %constant.21.clone.1), kind=kCustom, calls=%fused_computation.47 | custom fusion | bytes 49664 | tf_op jit(solution)/shard_map/scatter | solution.py:48
  46.1 0.8 all_to_all.13
  46.9 12.1 %all-to-all-start = ((s32[64,1,192]{2,1,0:T(1,128)}), s32[64,1,192]{2,1,0:T(1,128)S(1)}, u32[]{:S(2)}, u32[]{:S(2)}) async-start(s32[64,1,192]{2,1,0:T(1,128)} %all_to_all.13), calls=%async_computation | async-start | bytes 131072 | tf_op jit(solution)/shard_map/all_to_all | solution.py:53
  59.0 4.0 copy.28
  63.0 5.7 %all-to-all-done = s32[64,1,192]{2,1,0:T(1,128)S(1)} async-done(((s32[64,1,192]{2,1,0:T(1,128)}), s32[64,1,192]{2,1,0:T(1,128)S(1)}, u32[]{:S(2)}, u32[]{:S(2)}) %all-to-all-start) | async-done | bytes 49184 | tf_op jit(solution)/shard_map/all_to_all | solution.py:53
  69.0 48.5 %gather_fusion = bf16[12288,192]{1,0:T(8,128)(2,1)} fusion(bf16[8192,192]{1,0:T(8,128)(2,1)} %bitcast.38, s32[12288]{0:T(1024)S(1)} %broadcast_clamp_fusion), kind=kCustom, calls=%fused_computation | custom fusion | bytes 9486336 | tf_op jit(solution)/shard_map/jit(_take)/gather | solution.py:52
  117.6 7.6 %broadcast_select_fusion = bf16[64,192,192]{2,1,0:T(8,128)(2,1)} fusion(bf16[64,192,192]{2,1,0:T(8,128)(2,1)} %bitcast.39, pred[64,192]{1,0:T(8,128)(4,1)S(1)} %compare_and_fusion), kind=kLoop, calls=%fused_computation.3 | loop fusion | flops 2359296 | bytes 9449472 | tf_op jit(solution)/shard_map/jit(_take)/select_n | solution.py:52
  125.2 5.8 %all-to-all-start.1 = ((bf16[64,192,192]{2,1,0:T(8,128)(2,1)}), bf16[64,192,192]{2,1,0:T(8,128)(2,1)}, u32[]{:S(2)}, u32[]{:S(2)}) async-start(bf16[64,192,192]{2,1,0:T(8,128)(2,1)} %broadcast_select_fusion), calls=%async_computation.1 | async-start | bytes 12582912 | tf_op jit(solution)/shard_map/all_to_all | solution.py:55
  131.4 139.8 %all-to-all-done.1 = bf16[64,192,192]{2,1,0:T(8,128)(2,1)} async-done(((bf16[64,192,192]{2,1,0:T(8,128)(2,1)}), bf16[64,192,192]{2,1,0:T(8,128)(2,1)}, u32[]{:S(2)}, u32[]{:S(2)}) %all-to-all-start.1) | async-done | bytes 4718624 | tf_op jit(solution)/shard_map/all_to_all | solution.py:55
  271.2 34.5 %gather_fusion.1 = bf16[8192,192]{1,0:T(8,128)(2,1)} fusion(bf16[12288,192]{1,0:T(8,128)(2,1)} %bitcast.8, s32[8192]{0:T(1024)S(1)} %broadcast_clamp_fusion.1), kind=kCustom, calls=%fused_computation.1 | custom fusion | bytes 6324224 | tf_op jit(solution)/shard_map/jit(_take)/gather | solution.py:57
  305.7 7.7 %copy.29 = bf16[512,16,192]{0,2,1:T(8,128)(2,1)} copy(bf16[512,16,192]{2,1,0:T(8,128)(2,1)} %bitcast.40) | data formatting | bytes 6291456 | tf_op jit(solution)/shard_map/jit(_take)/gather | solution.py:57
  313.4 2.2 broadcast_select_fusion.1
  316.8 1.1 convolution_add_fusion
  317.9 13.0 %all_gather.11 = bf16[512,256]{1,0:T(8,128)(2,1)S(1)} all-gather(bf16[128,256]{1,0:T(8,128)(2,1)} %param.11), channel_id=1, replica_groups=mesh['wide'=64,'narrow'=4] {'narrow'}, dimensions={0}, use_global_device_ids=true | all-gather | bytes 327680 | tf_op jit(solution)/shard_map/all_gather | solution.py:70
  331.0 16.7 %all-gather.3.cloned.1.call-done = f32[2048,256]{1,0:T(8,128)} async-done(((f32[512,256]{1,0:T(8,128)}), f32[2048,256]{1,0:T(8,128)}) %all-gather.3.cloned.1.call-update) | async-done | bytes 2097168 | tf_op jit(solution)/shard_map/all_gather | solution.py:62
  347.7 2.6 reduce_sum.39
  350.2 2.2 fusion.5
  352.5 1.9 fusion.16
  354.3 0.9 fusion.13
  355.3 1.6 fusion.15
  356.9 182.2 %all-reduce.3.cloned.1.call-done = (f32[192,256]{1,0:T(8,128)}, f32[192,256]{1,0:T(8,128)}) async-done(((f32[192,256]{1,0:T(8,128)}, f32[192,256]{1,0:T(8,128)}), (f32[192,256]{1,0:T(8,128)}, f32[192,256]{1,0:T(8,128)})) %all-reduce.3.cloned.1.call-update) | async-done | bytes 393232 | tf_op jit(solution)/shard_map/psum | solution.py:74
  539.1 1.6 copy.39
  540.7 1.6 copy.40
  (28 shorter events, 2.1 us)
Async XLA Ops:
  7.2 308.9 %copy-start = (bf16[192,256]{1,0:T(8,128)(2,1)S(1)}, bf16[192,256]{1,0:T(8,128)(2,1)}, u32[]{:S(2)}) copy-start(bf16[192,256]{1,0:T(8,128)(2,1)} %param.9) | copy-start | bytes 294916
  7.2 51.8 %copy-start.2 = (bf16[192,8192]{1,0:T(8,128)(2,1)S(1)}, bf16[192,8192]{1,0:T(8,128)(2,1)}, u32[]{:S(2)}) copy-start(bf16[192,8192]{1,0:T(8,128)(2,1)} %param.6) | copy-start | bytes 9437188
  46.9 21.8 %all-to-all-start = ((s32[64,1,192]{2,1,0:T(1,128)}), s32[64,1,192]{2,1,0:T(1,128)S(1)}, u32[]{:S(2)}, u32[]{:S(2)}) async-start(s32[64,1,192]{2,1,0:T(1,128)} %all_to_all.13), calls=%async_computation | async-start | bytes 131072 | tf_op jit(solution)/shard_map/all_to_all | solution.py:53
  125.2 6.1 %copy-start.3 = (s32[512,16,1]{0,2,1:T(1,128)S(1)}, s32[512,16,1]{0,2,1:T(1,128)}, u32[]{:S(2)}) copy-start(s32[512,16,1]{0,2,1:T(1,128)} %param.7) | copy-start | bytes 98308
  125.2 146.0 %all-to-all-start.1 = ((bf16[64,192,192]{2,1,0:T(8,128)(2,1)}), bf16[64,192,192]{2,1,0:T(8,128)(2,1)}, u32[]{:S(2)}, u32[]{:S(2)}) async-start(bf16[64,192,192]{2,1,0:T(8,128)(2,1)} %broadcast_select_fusion), calls=%async_computation.1 | async-start | bytes 12582912 | tf_op jit(solution)/shard_map/all_to_all | solution.py:55
  131.0 216.6 %all-gather.3.cloned.1.call-start = ((), (), s32[]{:S(2)}) async-start(), calls=%async_computation.2 | async-start | bytes 2621440 | tf_op jit(solution)/shard_map/all_gather | solution.py:62
  315.6 1.2 copy-start.4
  316.0 0.7 copy-start.1
  317.9 221.2 %all-reduce.3.cloned.1.call-start = ((), (), s32[]{:S(2)}) async-start(), calls=%async_computation.3 | async-start | bytes 786432 | tf_op jit(solution)/shard_map/psum | solution.py:74
Sparse Core Ops, SparseCore 0:
  318.0 29.6 all-gather.2
  355.4 183.6 all-reduce.2
